TPU v7x, 256 devices: a whole 4x4x8 slice. The times are simulated.
256 devices in a mesh: row: 64 (over y, z, x_hi), col: 4 (over x_lo, core).
Axes of the slice: x: 4 (x_hi: 2, x_lo: 2; x = x_hi * 2 + x_lo), y: 4, z: 8, core: 2. Of those that a mesh axis runs over, the one named last changes fastest.
Arguments:
- matrix_slab: float32 [16384, 2048], P('row', 'col'), may hold values from -6 to 6
- sketch_matrix: float32 [144, 16384], P(None, 'row'), may hold values from -0.046875 to 0.046875
- pivots: int32 [1, 128], replicated, may hold values from 128 to 1919, as said below
Outputs:
- sketches: float32 [1, 144, 2048], P(None, None, 'col')
- q_panels: float32 [1, 16384, 128], P(None, 'row')
- r_factors: float32 [1, 128, 2048], P(None, None, 'col')
- first_factors: float32 [1, 128, 128], replicated
- slab_out: float32 [16384, 2048], P('row', 'col')
Inputs may be any that keep to these rules, and one draw needn't show every extreme that they name: `pivots`: each row holds 128 different numbers.
All inputs are finite; a program needn't handle non-finite values.
Results may differ from a plain program's by a relative error of at most 0.0003.
Values sent between devices are 32-bit elements; how exact they have to be, the bound alone decides.
A program may use at most 64 MiB of HBM per device.

v0:
```python
import math
import jax
import jax.numpy as jnp
from jax import lax
from jax.sharding import PartitionSpec as P

PANEL = 128


def product(left, right):
    return jnp.dot(left, right, precision=lax.Precision.HIGHEST, preferred_element_type=jnp.float32)


def solve_right(lower, rhs):
    return lax.linalg.triangular_solve(lower, rhs, left_side=False, lower=True, transpose_a=True)


def pick_columns(array, local_ids, inside):
    width = array.shape[1]
    picked = jnp.take(array, jnp.clip(local_ids, 0, width - 1), axis=1)
    return jnp.where(inside[None, :], picked, jnp.float32(0.0))


def place_columns(array, local_ids, inside, values):
    target = jnp.where(inside, local_ids, array.shape[1])
    return array.at[:, target].set(values, mode="drop")


def shards(matrix_slab, sketch_matrix, pivots):
    rows_dev, col_width = matrix_slab.shape
    m_total = rows_dev * lax.axis_size("row")
    row_scale = math.sqrt(m_total)
    col_first = lax.axis_index("col") * col_width
    column = col_first + jnp.arange(col_width, dtype=jnp.int32)
    current = matrix_slab
    sketch = lax.psum(product(sketch_matrix, current), "row")
    sketch_list = [sketch]
    pivot_ids = 0 + pivots[0]
    slot_ids = 0 + jnp.arange(PANEL, dtype=jnp.int32)
    pivot_local = pivot_ids - col_first
    slot_local = slot_ids - col_first
    pivot_inside = (pivot_local >= 0) & (pivot_local < col_width)
    slot_inside = (slot_local >= 0) & (slot_local < col_width)
    in_slots = (column >= 0) & (column < PANEL)
    panel_cols, lead_cols = lax.psum(
        (
            pick_columns(current, pivot_local, pivot_inside),
            pick_columns(current, slot_local, slot_inside),
        ),
        "col",
    )
    swapped = place_columns(
        place_columns(current, slot_local, slot_inside, panel_cols),
        pivot_local,
        pivot_inside,
        lead_cols,
    )
    gram_one = lax.psum(product(panel_cols.T, panel_cols), "row")
    factor_one = jnp.linalg.cholesky(gram_one)
    basis_one = solve_right(factor_one, panel_cols)
    gram_two = lax.psum(product(basis_one.T, basis_one), "row")
    factor_two = jnp.linalg.cholesky(gram_two)
    basis = solve_right(factor_two, basis_one)
    r_factor = product(factor_two.T, factor_one.T)
    projected = lax.psum(product(basis.T, swapped), "row")
    r_block = place_columns(projected, slot_local, slot_inside, r_factor)
    current = jnp.where(in_slots[None, :], jnp.float32(0.0), swapped - product(basis, projected))
    q_list = [basis * row_scale]
    r_list = [r_block / row_scale]
    first_list = [factor_one.T / row_scale]
    return (
        jnp.stack(sketch_list),
        jnp.stack(q_list),
        jnp.stack(r_list),
        jnp.stack(first_list),
        current,
    )


def solution(mesh):
    in_specs = (P("row", "col"), P(None, "row"), P())
    out_specs = (
        P(None, None, "col"),
        P(None, "row", None),
        P(None, None, "col"),
        P(),
        P("row", "col"),
    )
    return jax.shard_map(shards, mesh=mesh, in_specs=in_specs, out_specs=out_specs, check_vma=False)
```

profile of v0, /device:TPU:32, one launch (start us, length us, event | category | flops | bytes accessed | tf_op | source)
XLA Modules:
  0.0 1997.1 jit_solution(17937217708790303102)
XLA Ops:
  7.2 0.0 copy-start
  7.2 0.0 all-reduce.13.cloned.1.call-start
  7.2 0.7 copy-done.8
  8.0 1.2 copy.8
  9.2 0.8 gather_fusion
  10.0 0.8 gather_fusion.1
  10.8 0.8 bitcast_select_fusion.1
  11.5 0.8 bitcast_select_fusion
  12.3 0.0 all-reduce.13.cloned.1.call-update
  12.3 0.0 all-reduce.7.cloned.1.call-start
  12.4 44.1 %all-reduce.13.cloned.1.call-done = (f32[256,128]{0,1:T(8,128)}, f32[256,128]{0,1:T(8,128)}) async-done(((f32[256,128]{0,1:T(8,128)}, f32[256,128]{0,1:T(8,128)}), (f32[256,128]{0,1:T(8,128)}, f32[256,128]{0,1:T(8,128)})) %all-reduce.13.cloned.1.call-update) | async-done | bytes 262160 | tf_op jit(solution)/shard_map/psum | solution.py:45
  56.5 1.9 fusion.29
  58.4 0.0 all-reduce.7.cloned.1.call-update
  58.4 0.0 all-reduce.9.cloned.1.call-start
  58.5 619.8 %all-reduce.7.cloned.1.call-done = f32[128,128]{0,1:T(8,128)} async-done(((f32[128,128]{0,1:T(8,128)}), f32[128,128]{0,1:T(8,128)}) %all-reduce.7.cloned.1.call-update) | async-done | bytes 65552 | tf_op jit(solution)/shard_map/psum | solution.py:58
  678.2 1.0 copy.10
  679.3 11.7 cholesky.44
  691.0 0.0 copy-start.2
  691.0 0.6 compare_reduce_fusion.1
  691.7 0.7 multiply_bitcast_fusion.2
  692.3 9.8 custom-call.6
  702.2 0.3 convolution_bitcast_fusion.2
  702.5 0.9 fusion.30
  703.4 0.0 all-reduce.9.cloned.1.call-update
  703.4 0.0 all-reduce.11.cloned.1.call-start
  703.5 1.2 convolution_bitcast_fusion
  704.6 1.2 scatter_custom_fusion
  705.9 1.4 scatter_custom_fusion.1
  707.3 610.2 %all-reduce.9.cloned.1.call-done = f32[128,128]{0,1:T(8,128)} async-done(((f32[128,128]{0,1:T(8,128)}), f32[128,128]{0,1:T(8,128)}) %all-reduce.9.cloned.1.call-update) | async-done | bytes 65552 | tf_op jit(solution)/shard_map/psum | solution.py:61
  1317.6 1.0 copy.12
  1318.6 11.7 cholesky.55
  1330.4 0.7 compare_reduce_fusion
  1331.1 0.6 select_bitcast_fusion
  1331.7 9.8 custom-call.7
  1341.5 0.3 convolution_bitcast_fusion.1
  1341.8 1.3 fusion.31
  1343.2 0.0 all-reduce.11.cloned.1.call-update
  1343.2 0.2 copy.16
  1343.4 0.7 copy.19
  1344.2 0.8 copy.17
  1344.9 1.5 fusion.15
  1346.4 639.0 %all-reduce.11.cloned.1.call-done = (f32[1,144,512]{2,1,0:T(8,128)}, f32[128,512]{1,0:T(8,128)}) async-done(((f32[1,144,512]{2,1,0:T(8,128)}, f32[128,512]{1,0:T(8,128)}), (f32[1,144,512]{2,1,0:T(8,128)}, f32[128,512]{1,0:T(8,128)})) %all-reduce.11.cloned.1.call-update) | async-done | bytes 557072 | tf_op jit(solution)/shard_map/psum | solution.py:36
  1985.4 1.1 copy.15
  1986.5 1.0 scatter_fusion
  1987.5 0.8 copy.18
  1988.4 0.1 copy-done.3
  1988.5 1.4 fusion
  1989.9 0.7 copy.31
  (28 shorter events, 0.2 us)
Async XLA Ops:
  7.2 696.3 %copy-start = (f32[144,256]{1,0:T(8,128)S(1)}, f32[144,256]{1,0:T(8,128)}, u32[]{:S(2)}) copy-start(f32[144,256]{1,0:T(8,128)} %param.9) | copy-start | bytes 442372
  7.2 49.3 %all-reduce.13.cloned.1.call-start = ((), (), s32[]{:S(2)}) async-start(), calls=%async_computation.3 | async-start | bytes 524288 | tf_op jit(solution)/shard_map/psum | solution.py:45
  7.2 0.7 copy-start.8
  12.3 665.9 %all-reduce.7.cloned.1.call-start = ((), (), s32[]{:S(2)}) async-start(), calls=%async_computation | async-start | bytes 131072 | tf_op jit(solution)/shard_map/psum | solution.py:58
  58.4 1259.2 %all-reduce.9.cloned.1.call-start = ((), (), s32[]{:S(2)}) async-start(), calls=%async_computation.1 | async-start | bytes 131072 | tf_op jit(solution)/shard_map/psum | solution.py:61
  678.2 1.0 copy-start.6
  691.0 11.2 copy-start.1
  691.0 12.5 copy-start.2
  703.4 1282.0 %all-reduce.11.cloned.1.call-start = ((), (), s32[]{:S(2)}) async-start(), calls=%async_computation.2 | async-start | bytes 1114112 | tf_op jit(solution)/shard_map/psum | solution.py:36
  704.6 1.2 copy-start.7
  1317.6 1.0 copy-start.5
  1987.5 1.0 copy-start.3
  1988.5 1.4 copy-start.4
Sparse Core Ops, SparseCore 0:
  12.4 44.0 all-reduce.12
  59.9 618.3 all-reduce.6
  703.5 613.9 all-reduce.8
  1343.3 642.0 all-reduce.10
where the time goes:
time: 2000 us
  waiting for transfers between devices  1910 us (96%)
  other arithmetic  47.4 us (2%)
    psum x1, waiting for transfers between devices, shards(): sketch = lax.psum(product(sketch_matrix, current), 'row')  639 us
    psum x1, waiting for transfers between devices, shards(): gram_one = lax.psum(product(panel_cols.T, panel_cols), 'row')  620 us
    psum x1, waiting for transfers between devices, shards(): gram_two = lax.psum(product(basis_one.T, basis_one), 'row')  610 us
    psum x1, waiting for transfers between devices, shards(): lax.psum((pick_columns(current, pivot_local, pivot_inside), pick_columns(...  44.1 us
  transfers between devices with their start and end apart: 4, of which 4 were waited for; matrix products, arithmetic and copies ran while one was open for 0% of the time, Pallas kernels for 0%

commit v1 on v0

--- a/solution.py
+++ b/solution.py
@@ -58,7 +58,7 @@
     gram_one = lax.psum(product(panel_cols.T, panel_cols), "row")
     factor_one = jnp.linalg.cholesky(gram_one)
     basis_one = solve_right(factor_one, panel_cols)
-    gram_two = lax.psum(product(basis_one.T, basis_one), "row")
+    gram_two = jnp.sum(lax.all_gather(product(basis_one.T, basis_one), "row"), axis=0)
     factor_two = jnp.linalg.cholesky(gram_two)
     basis = solve_right(factor_two, basis_one)
     r_factor = product(factor_two.T, factor_one.T)

time: 2000 us -> 1510 us (0.76)
  waiting for transfers between devices: 1910 us -> 1420 us
    psum x1 -> x0, waiting for transfers between devices: 610 us -> none  [shards(): gram_two = lax.psum(product(basis_one.T, basis_one), 'row')]
    all_gather x0 -> x1, waiting for transfers between devices: none -> 120 us  [shards(): lax.all_gather(product(basis_one.T, basis_one), 'row')]
  transfers between devices with their start and end apart: 4 -> 4, of which waited for: 4 -> 4; matrix products, arithmetic and copies ran while one was open for 0% -> 1% of each run, Pallas kernels for 0% -> 0%
where the time goes in v1:
time: 1510 us
  waiting for transfers between devices  1420 us (94%)
  other arithmetic  52 us (3%)
    psum x1, waiting for transfers between devices, shards(): sketch = lax.psum(product(sketch_matrix, current), 'row')  639 us
    psum x1, waiting for transfers between devices, shards(): gram_one = lax.psum(product(panel_cols.T, panel_cols), 'row')  620 us
    all_gather x1, waiting for transfers between devices, shards(): lax.all_gather(product(basis_one.T, basis_one), 'row')  120 us
    psum x1, waiting for transfers between devices, shards(): lax.psum((pick_columns(current, pivot_local, pivot_inside), pick_columns(...  44.1 us
  transfers between devices with their start and end apart: 4, of which 4 were waited for; matrix products, arithmetic and copies ran while one was open for 1% of the time, Pallas kernels for 0%

profile of v1, /device:TPU:32, one launch (start us, length us, event | category | flops | bytes accessed | tf_op | source)
XLA Modules:
  0.0 1512.2 jit_solution(7402550568766089230)
XLA Ops:
  7.2 0.0 all-reduce.10.cloned.1.call-start
  7.3 0.7 and_bitcast_fusion
  8.0 0.7 compare_and_fusion.1
  8.7 1.2 copy.19
  10.0 0.8 gather_fusion.1
  10.7 0.8 gather_fusion
  11.5 0.8 bitcast_select_fusion
  12.2 0.8 bitcast_select_fusion.1
  13.0 0.0 all-reduce.10.cloned.1.call-update
  13.0 0.0 all-reduce.6.cloned.1.call-start
  13.1 44.1 %all-reduce.10.cloned.1.call-done = (f32[256,128]{0,1:T(8,128)}, f32[256,128]{0,1:T(8,128)}) async-done(((f32[256,128]{0,1:T(8,128)}, f32[256,128]{0,1:T(8,128)}), (f32[256,128]{0,1:T(8,128)}, f32[256,128]{0,1:T(8,128)})) %all-reduce.10.cloned.1.call-update) | async-done | bytes 262160 | tf_op jit(solution)/shard_map/psum | solution.py:45
  57.2 1.9 fusion.29
  59.1 0.0 all-reduce.6.cloned.1.call-update
  59.1 0.0 all-gather.3.cloned.1.call-start
  59.2 619.8 %all-reduce.6.cloned.1.call-done = f32[128,128]{0,1:T(8,128)} async-done(((f32[128,128]{0,1:T(8,128)}), f32[128,128]{0,1:T(8,128)}) %all-reduce.6.cloned.1.call-update) | async-done | bytes 65552 | tf_op jit(solution)/shard_map/psum | solution.py:58
  679.0 0.9 copy.21
  679.9 0.9 fusion.8
  680.8 11.7 cholesky.44
  692.5 0.6 compare_reduce_fusion.1
  693.1 0.7 multiply_bitcast_fusion.2
  693.8 9.8 custom-call.6
  703.6 1.2 convolution_bitcast_fusion.2
  704.8 0.9 fusion.30
  705.7 0.0 all-gather.3.cloned.1.call-update
  705.8 0.0 all-reduce.8.cloned.1.call-start
  705.8 1.2 convolution_bitcast_fusion
  707.0 1.6 scatter_custom_fusion
  708.6 1.8 scatter_custom_fusion.1
  710.4 120.2 %all-gather.3.cloned.1.call-done = f32[8192,128]{1,0:T(8,128)} async-done(((f32[128,128]{1,0:T(8,128)}), f32[8192,128]{1,0:T(8,128)}) %all-gather.3.cloned.1.call-update) | async-done | bytes 4194320 | tf_op jit(solution)/shard_map/all_gather | solution.py:61
  830.7 2.4 reduce_sum.9
  833.1 0.1 copy.22
  833.2 11.7 cholesky.55
  844.9 0.7 compare_reduce_fusion
  845.7 0.6 select_bitcast_fusion
  846.3 9.8 custom-call.7
  856.1 0.3 convolution_bitcast_fusion.1
  856.4 1.3 fusion.31
  857.8 0.0 all-reduce.8.cloned.1.call-update
  857.8 0.2 copy.26
  858.0 0.7 copy.29
  858.8 0.8 copy.27
  859.5 1.5 fusion.15
  861.0 638.5 %all-reduce.8.cloned.1.call-done = (f32[1,144,512]{2,1,0:T(8,128)}, f32[128,512]{1,0:T(8,128)}) async-done(((f32[1,144,512]{2,1,0:T(8,128)}, f32[128,512]{1,0:T(8,128)}), (f32[1,144,512]{2,1,0:T(8,128)}, f32[128,512]{1,0:T(8,128)})) %all-reduce.8.cloned.1.call-update) | async-done | bytes 557072 | tf_op jit(solution)/shard_map/psum | solution.py:36
  1499.5 1.1 copy.25
  1500.7 1.0 scatter_fusion
  1501.7 0.8 copy.28
  1502.5 2.4 fusion
  1504.9 0.7 copy.39
  (19 shorter events, 0.2 us)
Async XLA Ops:
  7.2 698.7 %copy-start = (f32[144,256]{1,0:T(8,128)S(1)}, f32[144,256]{1,0:T(8,128)}, u32[]{:S(2)}) copy-start(f32[144,256]{1,0:T(8,128)} %param.9) | copy-start | bytes 442372
  7.2 699.8 %copy-start.3 = (s32[1,128]{1,0:T(1,128)S(1)}, s32[1,128]{1,0:T(1,128)}, u32[]{:S(2)}) copy-start(s32[1,128]{1,0:T(1,128)} %param.10) | copy-start | bytes 1540
  7.2 698.6 %copy-start.1 = (f32[256,512]{1,0:T(8,128)S(1)}, f32[256,512]{1,0:T(8,128)}, u32[]{:S(2)}) copy-start(f32[256,512]{1,0:T(8,128)} %param.8) | copy-start | bytes 1572868
  7.2 50.0 %all-reduce.10.cloned.1.call-start = ((), (), s32[]{:S(2)}) async-start(), calls=%async_computation.3 | async-start | bytes 524288 | tf_op jit(solution)/shard_map/psum | solution.py:45
  13.0 665.9 %all-reduce.6.cloned.1.call-start = ((), (), s32[]{:S(2)}) async-start(), calls=%async_computation | async-start | bytes 131072 | tf_op jit(solution)/shard_map/psum | solution.py:58
  59.1 771.5 %all-gather.3.cloned.1.call-start = ((), (), s32[]{:S(2)}) async-start(), calls=%async_computation.1 | async-start | bytes 4259840 | tf_op jit(solution)/shard_map/all_gather | solution.py:61
  705.8 793.8 %all-reduce.8.cloned.1.call-start = ((), (), s32[]{:S(2)}) async-start(), calls=%async_computation.2 | async-start | bytes 1114112 | tf_op jit(solution)/shard_map/psum | solution.py:36
  1499.5 5.4 copy-start.2
Sparse Core Ops, SparseCore 0:
  13.2 44.0 all-reduce.9
  60.6 618.3 all-reduce.5
  705.9 124.7 all-gather.2
  857.9 641.5 all-reduce.7
